TPU v7x, 32 devices: a whole 2x2x4 slice. The times are simulated.
32 devices in a mesh: rows: 8 (over z, x), grp: 4 (over y, core).
Axes of the slice: x: 2, y: 2, z: 4, core: 2. Of those that a mesh axis runs over, the one named last changes fastest.
Arguments:
- matrix: float32 [65536, 1024], P(('rows', 'grp'))
- row_signs: int32 [65536], P(('rows', 'grp')), may hold values from -1 to 1, as said below
- samples: int32 [8192], P(('rows', 'grp')), may hold values from 0 to 65535, as said below
Outputs:
- factor: float32 [1024, 1024], P('rows')
Inputs may be any that keep to these rules, and one draw needn't show every extreme that they name: `row_signs`: every entry is 1 or -1. `samples`: entries are distinct and increasing; entries k * 256 to (k + 1) * 256 - 1 lie in rows k * 2048 to (k + 1) * 2048 - 1.
All inputs are finite; a program needn't handle non-finite values.
Results may differ from a plain program's by a relative error of at most 0.00011.
Values sent between devices are 32-bit elements; how exact they have to be, the bound alone decides.
A program may use at most 128 MiB of HBM per device.

v0:
```python
import jax
import jax.numpy as jnp
from jax import lax
from jax.sharding import PartitionSpec as P

exact_mode = lax.Precision.HIGHEST


def parity_sign(left, right, length):
    correlation = left & right
    ones_total = jnp.zeros_like(correlation)
    for bit_level in range(max(1, length.bit_length() - 1)):
        ones_total = ones_total + (correlation >> bit_level & 1)
    return (1 - 2 * (ones_total % 2)).astype(jnp.float32)


def sylvester(length):
    indices = jnp.arange(length, dtype=jnp.int32)
    return parity_sign(indices[:, None], indices[None, :], length)


def shards(matrix, row_signs, samples):
    count_rows = lax.axis_size("rows")
    count_grp = lax.axis_size("grp")
    blocks = count_rows * count_grp
    row_dev, col_count = matrix.shape
    piece_rows = row_dev // blocks
    total_rows = row_dev * blocks
    sample_dev = samples.shape[0]
    position = lax.axis_index(("rows", "grp"))
    signed = matrix * row_signs.astype(jnp.float32)[:, None]
    before = jnp.dot(sylvester(row_dev), signed, precision=exact_mode)
    arrived = lax.all_to_all(
        lax.all_to_all(
            before.reshape(1, 1, row_dev, col_count),
            "rows",
            split_axis=2,
            concat_axis=0,
            tiled=True,
        ),
        "grp",
        split_axis=2,
        concat_axis=1,
        tiled=True,
    )
    mixed_rows = jnp.dot(
        sylvester(blocks), arrived.reshape(blocks, piece_rows * col_count), precision=exact_mode
    )
    mixed_rows = mixed_rows.reshape(count_rows, count_grp, piece_rows, col_count)
    mixed_rows = mixed_rows / jnp.sqrt(jnp.float32(total_rows))
    all_indices = lax.all_gather(samples, ("rows", "grp"), axis=0, tiled=True)
    owner_block = all_indices // row_dev
    within = all_indices % row_dev - position * piece_rows
    owner_hit = (owner_block[:, None] == jnp.arange(blocks, dtype=jnp.int32)[None, :]).astype(
        jnp.float32
    )
    local_hit = (within[:, None] == jnp.arange(piece_rows, dtype=jnp.int32)[None, :]).astype(
        jnp.float32
    )
    weights = jnp.einsum("kb,kt->bt", owner_hit, local_hit, precision=exact_mode).reshape(
        blocks * piece_rows
    )
    flat_rows = mixed_rows.reshape(blocks * piece_rows, col_count)
    local_gram = jnp.einsum(
        "kn,km->nm", flat_rows * weights[:, None], flat_rows, precision=exact_mode
    )
    summed_gram = lax.psum(local_gram, ("rows", "grp"))
    gram_total = summed_gram * (total_rows / (sample_dev * blocks))
    lower_factor = jnp.linalg.cholesky(gram_total)
    upper_factor = lower_factor.T
    share_rows = col_count // count_rows
    return lax.dynamic_slice_in_dim(
        upper_factor, lax.axis_index("rows") * share_rows, share_rows, 0
    )


def solution(mesh):
    return jax.shard_map(
        shards,
        mesh=mesh,
        in_specs=(P(("rows", "grp"), None), P(("rows", "grp")), P(("rows", "grp"))),
        out_specs=P("rows", None),
        check_vma=False,
    )
```

profile of v0, /device:TPU:0, one launch (start us, length us, event | category | flops | bytes accessed | tf_op | source)
XLA Modules:
  0.0 873.1 jit_solution(1184886997414699403)
XLA Ops:
  7.2 4.0 fusion.115
  11.2 93.9 %fusion.26 = f32[1,1,2048,1024]{3,2,1,0:T(8,128)S(1)} fusion(f32[2048,1024]{1,0:T(8,128)S(1)} %fusion.115), kind=kOutput, calls=%fused_computation.29 | convolution fusion | flops 51736739840 | bytes 16777216 | tf_op jit(solution)/shard_map/dot_general | solution.py:32
  105.2 10.7 %copy.40 = f32[1,1,2048,1024]{3,1,0,2:T(1,128)S(1)} copy(f32[1,1,2048,1024]{3,2,1,0:T(8,128)S(1)} %fusion.26) | data formatting | bytes 16777216 | tf_op jit(solution)/shard_map/reshape | solution.py:35
  115.9 190.1 %all_to_all.21 = f32[1,1,2048,1024]{3,1,0,2:T(1,128)S(1)} all-to-all(f32[1,1,2048,1024]{3,1,0,2:T(1,128)S(1)} %copy.40), channel_id=1, replica_groups=mesh['rows'=8,'grp'=4] {'rows'}, dimensions={2} | all-to-all | bytes 16777216 | tf_op jit(solution)/shard_map/all_to_all | solution.py:34
  306.0 8.1 copy.41
  314.1 5.8 all-to-all-start.1
  320.0 123.8 %all-gather = s32[32,1,256]{2,1,0:T(1,128)S(1)} all-gather(s32[1,1,256]{2,1,0:T(1,128)S(1)} %bitcast.77), channel_id=1, replica_groups=mesh['rows'=8,'grp'=4] {'rows','grp'}, dimensions={0}, use_global_device_ids=true | all-gather | bytes 33792 | tf_op jit(solution)/shard_map/all_gather | solution.py:51
  444.5 11.4 %copy.42 = f32[8,1,256,1024]{3,2,0,1:T(8,128)} copy(f32[8,1,256,1024]{3,0,1,2:T(8,128)} %all-to-all-done.1) | data formatting | bytes 16777216 | tf_op jit(solution)/shard_map/all_to_all | solution.py:33
  456.0 7.5 reshape.191
  463.4 10.6 %fusion.9 = f32[8,4,64,1024]{3,0,2,1:T(8,128)S(1)} fusion(f32[4,64,8,1024]{3,2,1,0:T(8,128)} %bitcast.73, s32[8,4]{0,1:T(4,128)S(1)} %multiply_add_fusion), kind=kOutput, calls=%fused_computation.12 | convolution fusion | flops 805336064 | bytes 16777344 | tf_op jit(solution)/shard_map/dot_general | solution.py:46
  474.1 31.2 %fusion.35 = f32[1024,1024]{0,1:T(8,128)} fusion(f32[8,4,64,1024]{3,0,2,1:T(8,128)S(1)} %fusion.9, f32[8,4,64]{0,2,1:T(8,128)S(1)} %copy.44), kind=kOutput, calls=%fused_computation.35 | convolution fusion | flops 25773998080 | bytes 12591104 | tf_op jit(solution)/shard_map/kn,km->nm/dot_general | solution.py:64
  505.4 138.7 %all-reduce.3.cloned.1.call-done = f32[1024,1024]{0,1:T(8,128)} async-done(((f32[1024,1024]{0,1:T(8,128)}), f32[1024,1024]{0,1:T(8,128)}) %all-reduce.3.cloned.1.call-update) | async-done | bytes 4194320 | tf_op jit(solution)/shard_map/psum | solution.py:67
  644.0 5.0 broadcast_multiply_fusion
  649.0 5.3 copy.46
  654.4 4.4 fusion.31
  658.8 1.9 copy-done
  660.8 11.7 %cholesky.223 = f32[128,128]{1,0:T(8,128)S(1)} custom-call(f32[128,128]{1,0:T(8,128)S(1)} %cholesky.580), custom_call_target="Cholesky" | custom-call | tf_op jit(solution)/shard_map/jit(cholesky)/cholesky | solution.py:69
  672.5 2.5 cholesky.255
  675.0 9.8 %custom-call.59 = f32[1,128,128]{1,2,0:T(8,128)S(1)} custom-call(f32[1,128,128]{2,1,0:T(8,128)S(1)} %get-tuple-element.26), custom_call_target="InvertDiagBlocksLowerTriangular" | custom-call | tf_op jit(solution)/shard_map/jit(cholesky)/cholesky | solution.py:69
  684.8 2.4 constant_dynamic-update-slice_fusion.7
  687.2 1.5 convolution_subtract_fusion
  688.8 12.1 %cholesky.244 = f32[128,128]{1,0:T(8,128)S(1)} custom-call(f32[128,128]{1,0:T(8,128)S(1)} %cholesky.584), custom_call_target="Cholesky" | custom-call | tf_op jit(solution)/shard_map/jit(cholesky)/cholesky | solution.py:69
  701.5 9.8 %custom-call.60 = f32[1,128,128]{1,2,0:T(8,128)S(1)} custom-call(f32[1,128,128]{2,1,0:T(8,128)S(1)} %get-tuple-element.23), custom_call_target="InvertDiagBlocksLowerTriangular" | custom-call | tf_op jit(solution)/shard_map/jit(cholesky)/cholesky | solution.py:69
  711.3 1.2 convolution_dynamic-update-slice_fusion
  712.6 2.1 convolution_subtract_fusion.1
  714.7 11.7 %cholesky.468 = f32[128,128]{1,0:T(8,128)S(1)} custom-call(f32[128,128]{1,0:T(8,128)S(1)} %cholesky.589), custom_call_target="Cholesky" | custom-call | tf_op jit(solution)/shard_map/jit(cholesky)/cholesky | solution.py:69
  727.0 9.8 %custom-call.61 = f32[1,128,128]{1,2,0:T(8,128)S(1)} custom-call(f32[1,128,128]{2,1,0:T(8,128)S(1)} %get-tuple-element.20), custom_call_target="InvertDiagBlocksLowerTriangular" | custom-call | tf_op jit(solution)/shard_map/jit(cholesky)/cholesky | solution.py:69
  736.8 1.2 convolution_dynamic-update-slice_fusion.1
  738.0 2.3 convolution_subtract_fusion.2
  740.3 11.9 %cholesky.487 = f32[128,128]{1,0:T(8,128)S(1)} custom-call(f32[128,128]{1,0:T(8,128)S(1)} %cholesky.594), custom_call_target="Cholesky" | custom-call | tf_op jit(solution)/shard_map/jit(cholesky)/cholesky | solution.py:69
  752.9 9.8 %custom-call.62 = f32[1,128,128]{1,2,0:T(8,128)S(1)} custom-call(f32[1,128,128]{2,1,0:T(8,128)S(1)} %get-tuple-element.17), custom_call_target="InvertDiagBlocksLowerTriangular" | custom-call | tf_op jit(solution)/shard_map/jit(cholesky)/cholesky | solution.py:69
  762.7 1.1 convolution_dynamic-update-slice_fusion.2
  763.8 2.3 convolution_subtract_fusion.3
  766.1 11.7 %cholesky.506 = f32[128,128]{1,0:T(8,128)S(1)} custom-call(f32[128,128]{1,0:T(8,128)S(1)} %cholesky.599), custom_call_target="Cholesky" | custom-call | tf_op jit(solution)/shard_map/jit(cholesky)/cholesky | solution.py:69
  778.5 10.0 %custom-call.63 = f32[1,128,128]{1,2,0:T(8,128)S(1)} custom-call(f32[1,128,128]{2,1,0:T(8,128)S(1)} %get-tuple-element.14), custom_call_target="InvertDiagBlocksLowerTriangular" | custom-call | tf_op jit(solution)/shard_map/jit(cholesky)/cholesky | solution.py:69
  788.5 1.0 convolution_dynamic-update-slice_fusion.3
  789.5 2.3 convolution_subtract_fusion.4
  791.8 11.7 %cholesky.526 = f32[128,128]{1,0:T(8,128)S(1)} custom-call(f32[128,128]{1,0:T(8,128)S(1)} %cholesky.604), custom_call_target="Cholesky" | custom-call | tf_op jit(solution)/shard_map/jit(cholesky)/cholesky | solution.py:69
  804.2 9.8 %custom-call.64 = f32[1,128,128]{1,2,0:T(8,128)S(1)} custom-call(f32[1,128,128]{2,1,0:T(8,128)S(1)} %get-tuple-element.11), custom_call_target="InvertDiagBlocksLowerTriangular" | custom-call | tf_op jit(solution)/shard_map/jit(cholesky)/cholesky | solution.py:69
  814.0 0.9 convolution_dynamic-update-slice_fusion.4
  814.9 2.0 convolution_subtract_fusion.5
  817.0 11.7 %cholesky.546 = f32[128,128]{1,0:T(8,128)S(1)} custom-call(f32[128,128]{1,0:T(8,128)S(1)} %cholesky.609), custom_call_target="Cholesky" | custom-call | tf_op jit(solution)/shard_map/jit(cholesky)/cholesky | solution.py:69
  829.3 9.8 %custom-call.65 = f32[1,128,128]{1,2,0:T(8,128)S(1)} custom-call(f32[1,128,128]{2,1,0:T(8,128)S(1)} %get-tuple-element.8), custom_call_target="InvertDiagBlocksLowerTriangular" | custom-call | tf_op jit(solution)/shard_map/jit(cholesky)/cholesky | solution.py:69
  839.2 0.8 convolution_dynamic-update-slice_fusion.5
  840.0 1.8 convolution_subtract_fusion.6
  841.8 11.7 %cholesky.564 = f32[128,128]{1,0:T(8,128)S(1)} custom-call(f32[128,128]{1,0:T(8,128)S(1)} %convolution_subtract_fusion.6), custom_call_target="Cholesky" | custom-call | tf_op jit(solution)/shard_map/jit(cholesky)/cholesky | solution.py:69
  863.7 1.1 fusion.49
  864.8 1.0 copy.47
  (33 shorter events, 10.7 us)
Async XLA Ops:
  314.1 5.9 copy-start.1
  314.1 130.4 %all-to-all-start.1 = ((f32[8,1,256,1024]{3,0,1,2:T(8,128)}), f32[8,1,256,1024]{3,0,1,2:T(8,128)}, u32[]{:S(2)}, u32[]{:S(2)}) async-start(f32[8,1,256,1024]{3,0,1,2:T(8,128)} %copy.41), calls=%async_computation.1 | async-start | bytes 16777216 | tf_op jit(solution)/shard_map/all_to_all | solution.py:33
  319.9 324.1 %all-reduce.3.cloned.1.call-start = ((), (), s32[]{:S(2)}) async-start(), calls=%async_computation.2 | async-start | bytes 8388608 | tf_op jit(solution)/shard_map/psum | solution.py:67
  658.8 1.9 copy-start
Sparse Core Ops, SparseCore 0:
  505.5 138.4 all-reduce.2
where the time goes:
time: 885 us; the launch traced here: 873 us
  blocking collectives  314 us (35%)
  other arithmetic  188 us (21%)
  matrix products  159 us (18%)
  waiting for transfers between devices  139 us (16%)
  local copies, waits for them, and re-layouts  48.6 us (5%)
  between operations  19.1 us (2%)
    all_to_all x1, blocking collectives, shards(): lax.all_to_all(before.reshape(1, 1, row_dev, col_count), 'rows', split_ax...  190 us
    another operation x30, other arithmetic, shards(): lower_factor = jnp.linalg.cholesky(gram_total)  172 us
    psum x1, waiting for transfers between devices, shards(): summed_gram = lax.psum(local_gram, ('rows', 'grp'))  139 us
    all_gather x1, blocking collectives, shards(): all_indices = lax.all_gather(samples, ('rows', 'grp'), axis=0, tiled=True)  124 us
    dot_general x1, matrix products, shards(): before = jnp.dot(sylvester(row_dev), signed, precision=exact_mode)  93.9 us
    dot_general x1, matrix products, shards(): jnp.einsum('kn,km->nm', flat_rows * weights[:, None], flat_rows, precisio...  31.2 us
    another operation x14, matrix products, shards(): lower_factor = jnp.linalg.cholesky(gram_total)  23.1 us
  transfers between devices with their start and end apart: 2, of which 1 were waited for; matrix products, arithmetic and copies ran while one was open for 0% of the time, Pallas kernels for 0%

commit v1 on v0

--- a/solution.py
+++ b/solution.py
@@ -31,12 +31,18 @@
     signed = matrix * row_signs.astype(jnp.float32)[:, None]
     before = jnp.dot(sylvester(row_dev), signed, precision=exact_mode)
     arrived = lax.all_to_all(
-        lax.all_to_all(
-            before.reshape(1, 1, row_dev, col_count),
-            "rows",
-            split_axis=2,
-            concat_axis=0,
-            tiled=True,
+        jnp.concatenate(
+            lax.all_to_all(
+                jnp.stack(
+                    jnp.split(
+                        before.reshape(1, 1, row_dev, col_count), lax.axis_size("rows"), axis=2
+                    )
+                ),
+                "rows",
+                0,
+                0,
+            ),
+            axis=0,
         ),
         "grp",
         split_axis=2,

time: 885 us -> 875 us (0.989)
  local copies, waits for them, and re-layouts: 48.6 us -> 38.5 us
    all_to_all x2 -> x1, local copies, waits for them, and re-layouts: 19.5 us -> 11.4 us  [shards(): lax.all_to_all(jnp.concatenate(lax.all_to_all(jnp.stack(jnp.split(before....]
where the time goes in v1:
time: 875 us; the launch traced here: 863 us
  blocking collectives  314 us (36%)
  other arithmetic  188 us (21%)
  matrix products  160 us (18%)
  waiting for transfers between devices  139 us (16%)
  local copies, waits for them, and re-layouts  38.5 us (4%)
  between operations  19 us (2%)
    all_to_all x1, blocking collectives, shards(): lax.all_to_all(jnp.stack(jnp.split(before.reshape(1, 1, row_dev, col_coun...  190 us
    another operation x30, other arithmetic, shards(): lower_factor = jnp.linalg.cholesky(gram_total)  172 us
    psum x1, waiting for transfers between devices, shards(): summed_gram = lax.psum(local_gram, ('rows', 'grp'))  139 us
    all_gather x1, blocking collectives, shards(): all_indices = lax.all_gather(samples, ('rows', 'grp'), axis=0, tiled=True)  124 us
    dot_general x1, matrix products, shards(): before = jnp.dot(sylvester(row_dev), signed, precision=exact_mode)  94.3 us
    dot_general x1, matrix products, shards(): jnp.einsum('kn,km->nm', flat_rows * weights[:, None], flat_rows, precisio...  31.2 us
    another operation x14, matrix products, shards(): lower_factor = jnp.linalg.cholesky(gram_total)  23.1 us
  transfers between devices with their start and end apart: 2, of which 1 were waited for; matrix products, arithmetic and copies ran while one was open for 0% of the time, Pallas kernels for 0%

profile of v1, /device:TPU:0, one launch (start us, length us, event | category | flops | bytes accessed | tf_op | source)
XLA Modules:
  0.0 863.2 jit_solution(403141761070589356)
XLA Ops:
  7.2 4.0 fusion.123
  11.2 94.3 %fusion.26 = f32[1,1,2048,1024]{3,2,1,0:T(8,128)S(1)} fusion(f32[2048,1024]{1,0:T(8,128)S(1)} %fusion.123), kind=kOutput, calls=%fused_computation.29 | convolution fusion | flops 51736739840 | bytes 16777216 | tf_op jit(solution)/shard_map/dot_general | solution.py:32
  106.1 190.1 %all_to_all.14 = f32[8,1,1,256,1024]{4,3,2,1,0:T(8,128)S(1)} all-to-all(f32[8,1,1,256,1024]{4,3,2,1,0:T(8,128)S(1)} %fusion.43), channel_id=1, replica_groups=mesh['rows'=8,'grp'=4] {'rows'}, dimensions={0} | all-to-all | bytes 16777216 | tf_op jit(solution)/shard_map/all_to_all | solution.py:35
  296.3 8.1 copy.37
  304.3 5.8 all-to-all-start.1
  310.2 123.8 %all-gather = s32[32,1,256]{2,1,0:T(1,128)S(1)} all-gather(s32[1,1,256]{2,1,0:T(1,128)S(1)} %bitcast.109), channel_id=1, replica_groups=mesh['rows'=8,'grp'=4] {'rows','grp'}, dimensions={0}, use_global_device_ids=true | all-gather | bytes 33792 | tf_op jit(solution)/shard_map/all_gather | solution.py:57
  434.8 11.4 %copy.38 = f32[8,1,256,1024]{3,2,0,1:T(8,128)} copy(f32[8,1,256,1024]{3,0,1,2:T(8,128)} %all-to-all-done.1) | data formatting | bytes 16777216 | tf_op jit(solution)/shard_map/all_to_all | solution.py:33
  446.2 7.5 reshape.192
  453.7 10.6 %fusion.9 = f32[8,4,64,1024]{3,0,2,1:T(8,128)S(1)} fusion(f32[4,64,8,1024]{3,2,1,0:T(8,128)} %bitcast.105, s32[8,4]{0,1:T(4,128)S(1)} %multiply_add_fusion), kind=kOutput, calls=%fused_computation.12 | convolution fusion | flops 805336064 | bytes 16777344 | tf_op jit(solution)/shard_map/dot_general | solution.py:52
  464.3 31.2 %fusion.35 = f32[1024,1024]{0,1:T(8,128)} fusion(f32[8,4,64,1024]{3,0,2,1:T(8,128)S(1)} %fusion.9, f32[8,4,64]{0,2,1:T(8,128)S(1)} %copy.40), kind=kOutput, calls=%fused_computation.35 | convolution fusion | flops 25773998080 | bytes 12591104 | tf_op jit(solution)/shard_map/kn,km->nm/dot_general | solution.py:70
  495.6 138.5 %all-reduce.3.cloned.1.call-done = f32[1024,1024]{0,1:T(8,128)} async-done(((f32[1024,1024]{0,1:T(8,128)}), f32[1024,1024]{0,1:T(8,128)}) %all-reduce.3.cloned.1.call-update) | async-done | bytes 4194320 | tf_op jit(solution)/shard_map/psum | solution.py:73
  634.1 5.0 broadcast_multiply_fusion
  639.1 5.3 copy.42
  644.4 4.4 fusion.31
  648.9 1.9 copy-done
  650.8 11.7 %cholesky.223 = f32[128,128]{1,0:T(8,128)S(1)} custom-call(f32[128,128]{1,0:T(8,128)S(1)} %cholesky.580), custom_call_target="Cholesky" | custom-call | tf_op jit(solution)/shard_map/jit(cholesky)/cholesky | solution.py:75
  662.6 9.8 %custom-call.59 = f32[1,128,128]{1,2,0:T(8,128)S(1)} custom-call(f32[1,128,128]{2,1,0:T(8,128)S(1)} %get-tuple-element.26), custom_call_target="InvertDiagBlocksLowerTriangular" | custom-call | tf_op jit(solution)/shard_map/jit(cholesky)/cholesky | solution.py:75
  672.4 2.5 cholesky.255
  674.9 2.4 constant_dynamic-update-slice_fusion.7
  677.3 1.5 convolution_subtract_fusion
  678.8 12.1 %cholesky.244 = f32[128,128]{1,0:T(8,128)S(1)} custom-call(f32[128,128]{1,0:T(8,128)S(1)} %cholesky.584), custom_call_target="Cholesky" | custom-call | tf_op jit(solution)/shard_map/jit(cholesky)/cholesky | solution.py:75
  691.6 9.8 %custom-call.60 = f32[1,128,128]{1,2,0:T(8,128)S(1)} custom-call(f32[1,128,128]{2,1,0:T(8,128)S(1)} %get-tuple-element.23), custom_call_target="InvertDiagBlocksLowerTriangular" | custom-call | tf_op jit(solution)/shard_map/jit(cholesky)/cholesky | solution.py:75
  701.4 1.2 convolution_dynamic-update-slice_fusion
  702.6 2.1 convolution_subtract_fusion.1
  704.7 11.7 %cholesky.468 = f32[128,128]{1,0:T(8,128)S(1)} custom-call(f32[128,128]{1,0:T(8,128)S(1)} %cholesky.589), custom_call_target="Cholesky" | custom-call | tf_op jit(solution)/shard_map/jit(cholesky)/cholesky | solution.py:75
  717.7 9.8 %custom-call.61 = f32[1,128,128]{1,2,0:T(8,128)S(1)} custom-call(f32[1,128,128]{2,1,0:T(8,128)S(1)} %get-tuple-element.20), custom_call_target="InvertDiagBlocksLowerTriangular" | custom-call | tf_op jit(solution)/shard_map/jit(cholesky)/cholesky | solution.py:75
  727.5 1.2 convolution_dynamic-update-slice_fusion.1
  728.7 2.3 convolution_subtract_fusion.2
  731.0 11.9 %cholesky.487 = f32[128,128]{1,0:T(8,128)S(1)} custom-call(f32[128,128]{1,0:T(8,128)S(1)} %cholesky.594), custom_call_target="Cholesky" | custom-call | tf_op jit(solution)/shard_map/jit(cholesky)/cholesky | solution.py:75
  744.2 9.8 %custom-call.62 = f32[1,128,128]{1,2,0:T(8,128)S(1)} custom-call(f32[1,128,128]{2,1,0:T(8,128)S(1)} %get-tuple-element.17), custom_call_target="InvertDiagBlocksLowerTriangular" | custom-call | tf_op jit(solution)/shard_map/jit(cholesky)/cholesky | solution.py:75
  754.0 1.1 convolution_dynamic-update-slice_fusion.2
  755.1 2.3 convolution_subtract_fusion.3
  757.5 11.7 %cholesky.506 = f32[128,128]{1,0:T(8,128)S(1)} custom-call(f32[128,128]{1,0:T(8,128)S(1)} %cholesky.599), custom_call_target="Cholesky" | custom-call | tf_op jit(solution)/shard_map/jit(cholesky)/cholesky | solution.py:75
  770.5 10.0 %custom-call.63 = f32[1,128,128]{1,2,0:T(8,128)S(1)} custom-call(f32[1,128,128]{2,1,0:T(8,128)S(1)} %get-tuple-element.14), custom_call_target="InvertDiagBlocksLowerTriangular" | custom-call | tf_op jit(solution)/shard_map/jit(cholesky)/cholesky | solution.py:75
  780.5 1.0 convolution_dynamic-update-slice_fusion.3
  781.5 2.3 convolution_subtract_fusion.4
  783.8 11.7 %cholesky.526 = f32[128,128]{1,0:T(8,128)S(1)} custom-call(f32[128,128]{1,0:T(8,128)S(1)} %cholesky.604), custom_call_target="Cholesky" | custom-call | tf_op jit(solution)/shard_map/jit(cholesky)/cholesky | solution.py:75
  796.8 9.8 %custom-call.64 = f32[1,128,128]{1,2,0:T(8,128)S(1)} custom-call(f32[1,128,128]{2,1,0:T(8,128)S(1)} %get-tuple-element.11), custom_call_target="InvertDiagBlocksLowerTriangular" | custom-call | tf_op jit(solution)/shard_map/jit(cholesky)/cholesky | solution.py:75
  806.6 0.9 convolution_dynamic-update-slice_fusion.4
  807.5 2.0 convolution_subtract_fusion.5
  809.6 11.9 %cholesky.546 = f32[128,128]{1,0:T(8,128)S(1)} custom-call(f32[128,128]{1,0:T(8,128)S(1)} %cholesky.609), custom_call_target="Cholesky" | custom-call | tf_op jit(solution)/shard_map/jit(cholesky)/cholesky | solution.py:75
  822.8 9.8 %custom-call.65 = f32[1,128,128]{1,2,0:T(8,128)S(1)} custom-call(f32[1,128,128]{2,1,0:T(8,128)S(1)} %get-tuple-element.8), custom_call_target="InvertDiagBlocksLowerTriangular" | custom-call | tf_op jit(solution)/shard_map/jit(cholesky)/cholesky | solution.py:75
  832.6 0.8 convolution_dynamic-update-slice_fusion.5
  833.4 1.8 convolution_subtract_fusion.6
  835.2 11.7 %cholesky.564 = f32[128,128]{1,0:T(8,128)S(1)} custom-call(f32[128,128]{1,0:T(8,128)S(1)} %convolution_subtract_fusion.6), custom_call_target="Cholesky" | custom-call | tf_op jit(solution)/shard_map/jit(cholesky)/cholesky | solution.py:75
  847.6 0.7 compare_reduce_fusion
  853.8 1.1 fusion.57
  854.9 1.0 copy.43
  (40 shorter events, 10.4 us)
Async XLA Ops:
  304.3 5.9 copy-start.1
  304.3 130.4 %all-to-all-start.1 = ((f32[8,1,256,1024]{3,0,1,2:T(8,128)}), f32[8,1,256,1024]{3,0,1,2:T(8,128)}, u32[]{:S(2)}, u32[]{:S(2)}) async-start(f32[8,1,256,1024]{3,0,1,2:T(8,128)} %copy.37), calls=%async_computation.1 | async-start | bytes 16777216 | tf_op jit(solution)/shard_map/all_to_all | solution.py:33
  310.1 324.0 %all-reduce.3.cloned.1.call-start = ((), (), s32[]{:S(2)}) async-start(), calls=%async_computation.2 | async-start | bytes 8388608 | tf_op jit(solution)/shard_map/psum | solution.py:73
  648.9 1.9 copy-start
Sparse Core Ops, SparseCore 0:
  495.7 138.3 all-reduce.2
